TPU v7x, 32 devices: a whole 2x2x4 slice. The times are simulated.
32 devices in a mesh: row: 8 (over z, core), col: 4 (over y, x).
Axes of the slice: x: 2, y: 2, z: 4, core: 2. Of those that a mesh axis runs over, the one named last changes fastest.
Arguments:
- points: bfloat16 [2048, 1024], P(('row', 'col')), may hold values from -6 to 6
- factor: float32 [2048, 256], P(('row', 'col')), may hold values from 0 to 1
Outputs:
- factor_out: float32 [2048, 256], P(('row', 'col'))
All inputs are finite; a program needn't handle non-finite values.
Results may differ from a plain program's by a relative error of at most 0.002.
The roundings to bfloat16 on the way count: a program that leaves them out, or rounds other values in their place, can miss the bound.
Values may be sent and summed in bfloat16 or wider, within the bound.
A program may use at most 64 MiB of HBM per device.

v0:
```python
import math

import jax
import jax.numpy as jnp
from jax import lax
from jax.sharding import PartitionSpec as P

EMBED_WIDTH = 1024
ITERS = 2


def shards(points, factor):
    nrow = lax.axis_size("row")
    ncol = lax.axis_size("col")
    pts = points.shape[0]
    rank = factor.shape[1]
    total = pts * nrow * ncol
    row_pts = lax.all_gather(points, "col", axis=0, tiled=True)
    col_pts = lax.all_gather(points, "row", axis=0, tiled=True)
    gram_matrix = lax.dot_general(
        row_pts, col_pts, (((1,), (1,)), ((), ())), preferred_element_type=jnp.float32
    )
    row_sq = jnp.sum(jnp.square(row_pts.astype(jnp.float32)), axis=1)
    col_sq = jnp.sum(jnp.square(col_pts.astype(jnp.float32)), axis=1)
    kern = jnp.exp((2.0 * gram_matrix - row_sq[:, None] - col_sq[None, :]) * (0.5 / EMBED_WIDTH))
    row_sum, band = lax.psum((jnp.sum(kern, axis=1), jnp.sum(kern)), "col")
    col_sum, grand = lax.psum((jnp.sum(kern, axis=0), band), "row")
    affinity = (
        kern - row_sum[:, None] / total - col_sum[None, :] / total + grand / (total * total)
    ).astype(jnp.bfloat16)
    unit = 2.0 / math.sqrt(total * rank)
    h = factor * unit
    for step in range(ITERS):
        hb = h.astype(jnp.bfloat16)
        copies = lax.all_gather(hb, "row", axis=0, tiled=True)
        ah = lax.psum_scatter(
            jnp.dot(affinity, copies, preferred_element_type=jnp.float32),
            "col",
            scatter_dimension=0,
            tiled=True,
        )
        local_gram = lax.dot_general(
            h, h, (((0,), (0,)), ((), ())), precision=lax.Precision.HIGHEST
        )
        hh = lax.psum(local_gram, ("row", "col"))
        scale = 0.5 / jnp.sqrt(jnp.sum(hh * hh) + 1e-06)
        h = jnp.maximum(h - scale * (jnp.dot(h, hh, precision=lax.Precision.HIGHEST) - ah), 0.0)
    return h / unit


def solution(mesh):
    in_specs = (P(("row", "col"), None), P(("row", "col"), None))
    out_specs = P(("row", "col"), None)
    return jax.shard_map(shards, mesh=mesh, in_specs=in_specs, out_specs=out_specs, check_vma=False)
```

profile of v0, /device:TPU:1, one launch (start us, length us, event | category | flops | bytes accessed | tf_op | source)
XLA Modules:
  0.0 299.5 jit_solution(7194826416192646812)
XLA Ops:
  7.4 0.0 all-gather.2.cloned.1.call-start
  7.4 0.7 all-gather.2.cloned.1.call-update
  8.1 0.0 all-reduce.5.cloned.1.call-start
  8.1 2.0 fusion.12
  10.2 0.0 all-reduce.5.cloned.1.call-update
  10.2 0.0 reduce-scatter.3.cloned.1.call-start
  10.3 9.8 %all_gather.12 = bf16[256,1024]{1,0:T(8,128)(2,1)S(1)} all-gather(bf16[64,1024]{1,0:T(8,128)(2,1)} %param.2), channel_id=1, replica_groups=mesh['row'=8,'col'=4] {'col'}, dimensions={0}, use_global_device_ids=true | all-gather | bytes 655360 | tf_op jit(solution)/shard_map/all_gather | solution.py:18
  20.0 0.0 copy-done.1
  20.1 0.2 multiply_reduce_fusion.1
  20.2 17.2 %all_gather.14 = bf16[512,256]{1,0:T(8,128)(2,1)S(1)} all-gather(bf16[64,256]{1,0:T(8,128)(2,1)S(1)} %multiply_convert_fusion), channel_id=1, replica_groups=mesh['row'=8,'col'=4] {'row'}, dimensions={0}, use_global_device_ids=true | all-gather | bytes 294912 | tf_op jit(solution)/shard_map/all_gather | solution.py:35
  37.4 1.6 multiply_reduce_fusion
  39.0 0.0 copy-done
  39.0 1.2 fusion.20
  40.2 7.6 %all-reduce.1 = (f32[]{:T(128)}, f32[256]{0:T(256)S(1)}) all-reduce(f32[]{:T(128)} %get-tuple-element.6, f32[256]{0:T(256)S(1)} %get-tuple-element.5), channel_id=1, replica_groups=mesh['row'=8,'col'=4] {'col'}, use_global_device_ids=true, to_apply=%region_9.0 | all-reduce | flops 257 | bytes 2056 | tf_op jit(solution)/shard_map/psum | solution.py:26
  47.8 15.8 %all-reduce = (f32[]{:T(128)}, f32[512]{0:T(512)S(1)}) all-reduce(f32[]{:T(128)} %get-tuple-element.10, f32[512]{0:T(512)S(1)} %get-tuple-element.7), channel_id=1, replica_groups=mesh['row'=8,'col'=4] {'row'}, use_global_device_ids=true, to_apply=%region_10.0 | all-reduce | flops 513 | bytes 4104 | tf_op jit(solution)/shard_map/psum | solution.py:27
  64.3 1.0 fusion.19
  65.2 0.0 reduce-scatter.3.cloned.1.call-update
  65.3 0.0 all-reduce.7.cloned.1.call-start
  65.3 78.9 %all-reduce.5.cloned.1.call-done = f32[256,256]{1,0:T(8,128)} async-done(((f32[256,256]{1,0:T(8,128)}), f32[256,256]{1,0:T(8,128)}) %all-reduce.5.cloned.1.call-update) | async-done | bytes 262160 | tf_op jit(solution)/shard_map/psum | solution.py:45
  144.2 1.6 multiply_reduce_fusion.3
  146.5 0.0 reduce-scatter.3.cloned.1.call-done
  146.5 1.2 fusion.21
  147.7 15.5 %all_gather.15 = bf16[512,256]{1,0:T(8,128)(2,1)S(1)} all-gather(bf16[64,256]{1,0:T(8,128)(2,1)S(1)} %get-tuple-element.13), channel_id=1, replica_groups=mesh['row'=8,'col'=4] {'row'}, dimensions={0}, use_global_device_ids=true | all-gather | bytes 294912 | tf_op jit(solution)/shard_map/all_gather | solution.py:35
  163.2 1.1 fusion.22
  164.4 0.0 all-reduce.7.cloned.1.call-update
  164.4 0.0 reduce-scatter.5.cloned.1.call-start
  164.4 1.0 fusion.18
  165.4 0.0 reduce-scatter.5.cloned.1.call-update
  165.4 122.8 %all-reduce.7.cloned.1.call-done = f32[256,256]{1,0:T(8,128)} async-done(((f32[256,256]{1,0:T(8,128)}), f32[256,256]{1,0:T(8,128)}) %all-reduce.7.cloned.1.call-update) | async-done | bytes 262160 | tf_op jit(solution)/shard_map/psum | solution.py:45
  288.2 1.6 multiply_reduce_fusion.2
  290.5 0.0 reduce-scatter.5.cloned.1.call-done
  290.6 1.8 fusion.7
  (6 shorter events, 0.0 us)
Async XLA Ops:
  7.4 12.7 %copy-start.1 = (f32[64,256]{1,0:T(8,128)S(1)}, f32[64,256]{1,0:T(8,128)}, u32[]{:S(2)}) copy-start(f32[64,256]{1,0:T(8,128)} %param.3) | copy-start | bytes 196612
  7.4 30.1 %all-gather.2.cloned.1.call-start = ((), (), s32[]{:S(2)}) async-start(), calls=%async_computation.3 | async-start | bytes 1179648 | tf_op jit(solution)/shard_map/all_gather | solution.py:19
  8.1 136.1 %all-reduce.5.cloned.1.call-start = ((), (), s32[]{:S(2)}) async-start(), calls=%async_computation.2 | async-start | bytes 524288 | tf_op jit(solution)/shard_map/psum | solution.py:45
  10.2 136.3 %reduce-scatter.3.cloned.1.call-start = ((), (), s32[]{:S(2)}) async-start(), calls=%async_computation.4 | async-start | bytes 327680 | tf_op jit(solution)/shard_map/reduce_scatter | solution.py:36
  37.4 1.6 copy-start
  65.3 223.0 %all-reduce.7.cloned.1.call-start = ((), (), s32[]{:S(2)}) async-start(), calls=%async_computation.5 | async-start | bytes 524288 | tf_op jit(solution)/shard_map/psum | solution.py:45
  164.4 126.2 %reduce-scatter.5.cloned.1.call-start = ((), (), s32[]{:S(2)}) async-start(), calls=%async_computation.6 | async-start | bytes 327680 | tf_op jit(solution)/shard_map/reduce_scatter | solution.py:36
Sparse Core Ops, SparseCore 0:
  9.8 25.9 all-gather.1
  65.4 21.8 reduce-scatter.2
  167.9 22.5 reduce-scatter.4
Sparse Core Ops, SparseCore 1:
  14.1 130.1 all-reduce.4
  164.5 123.7 all-reduce.6
where the time goes:
time: 301 us; the launch traced here: 300 us
  waiting for transfers between devices  202 us (67%)
  blocking collectives  65.8 us (22%)
  between operations  16.6 us (6%)
  matrix products  9.39 us (3%)
  other arithmetic  5.03 us (2%)
    psum x2, waiting for transfers between devices, shards(): hh = lax.psum(local_gram, ('row', 'col'))  202 us
    all_gather x2, blocking collectives, shards(): copies = lax.all_gather(hb, 'row', axis=0, tiled=True)  32.7 us
    psum x1, blocking collectives, shards(): col_sum, grand = lax.psum((jnp.sum(kern, axis=0), band), 'row')  15.8 us
    all_gather x1, blocking collectives, shards(): row_pts = lax.all_gather(points, 'col', axis=0, tiled=True)  9.77 us
    psum x1, blocking collectives, shards(): row_sum, band = lax.psum((jnp.sum(kern, axis=1), jnp.sum(kern)), 'col')  7.59 us
  transfers between devices with their start and end apart: 5, of which 2 were waited for; matrix products, arithmetic and copies ran while one was open for 3% of the time, Pallas kernels for 0%

commit v1 on v0

v1 whole, which is shorter than its diff:
```python
import functools
import math

import jax
import jax.numpy as jnp
from jax import lax
from jax.experimental import pallas as pl
from jax.experimental.pallas import tpu as pltpu
from jax.sharding import PartitionSpec as P

MESH = pl.DeviceIdType.MESH


def kernel(nrow, ncol, side, pts_ref, fac_ref, out_ref, buf, hbuf, kern, aff, mg, ssem, rsem, hssem, hrsem, mssem, mrsem):
    nz, plane = nrow // 2, ncol
    nchips = nz * plane
    rows, width = pts_ref.shape
    rank = fac_ref.shape[1]
    total = rows * nrow * ncol
    unit = 2.0 / math.sqrt(total * rank)
    row, col = lax.axis_index("row"), lax.axis_index("col")
    z, core = row // 2, row % 2
    y, x = col // side, col % side
    own = z * plane + col

    def chip_of(kz, ka, kb, sign):
        ky = ka * (1 - core) + kb * core
        kx = ka * core + kb * (1 - core)
        zz = (z + sign * kz + nz) % nz
        yy = (y + sign * ky + side) % side
        xx = (x + sign * kx + side) % side
        return zz, yy * side + xx

    def number(kz, ka, kb):
        return (kz * side + ka) * side + kb

    def slot_of(kz, ka, kb):
        zz, cc = chip_of(kz, ka, kb, -1)
        return zz * plane + cc

    barrier = pltpu.get_barrier_semaphore()
    peers = [(kz, 0, 0) for kz in range(1, nz)] + [(0, k, 0) for k in range(1, side)] + [(0, 0, k) for k in range(1, side)]
    for peer in peers:
        zz, cc = chip_of(*peer, 1)
        pl.semaphore_signal(barrier, inc=1, device_id=(zz * 2 + core, cc), device_id_type=MESH)
    pl.semaphore_signal(barrier, inc=1, device_id=(z * 2 + 1 - core, col), device_id_type=MESH)

    h = fac_ref[...] * unit
    buf[own, core, :, :width] = pts_ref[...]
    buf[own, core, :, width:] = h.astype(jnp.bfloat16)
    pl.semaphore_wait(barrier, len(peers) + 1)

    def gather(ref, send_sem, recv_sem, ready):
        started = []

        def copy(source, number_there, device):
            block = ref.at[source, core]
            return pltpu.make_async_remote_copy(
                src_ref=block,
                dst_ref=block,
                send_sem=send_sem.at[number_there],
                recv_sem=recv_sem.at[number_there],
                device_id=device,
                device_id_type=MESH,
            )

        def send(source, number_there, device):
            op = copy(source, number_there, device)
            op.start()
            started.append(op)

        def arrive(slot, core_there, number_here):
            block = ref.at[slot, core_there]
            pltpu.make_async_remote_copy(
                src_ref=block,
                dst_ref=block,
                send_sem=send_sem.at[number_here],
                recv_sem=recv_sem.at[number_here],
                device_id=(z * 2 + 1 - core, col),
                device_id_type=MESH,
            ).wait_recv()

        def handle(kz, ka, kb):
            source = slot_of(kz, ka, kb)
            if kz or ka or kb:
                arrive(source, core, number(kz, ka, kb))
            if not (kz or ka or kb):
                for k in range(1, nz):
                    zz, cc = chip_of(k, 0, 0, 1)
                    send(source, number(k, 0, 0), (zz * 2 + core, cc))
            if not kb:
                if not ka:
                    for k in range(1, side):
                        zz, cc = chip_of(0, k, 0, 1)
                        send(source, number(kz, k, 0), (zz * 2 + core, cc))
                for k in range(1, side):
                    zz, cc = chip_of(0, 0, k, 1)
                    send(source, number(kz, ka, k), (zz * 2 + core, cc))
            send(source, nchips + number(kz, ka, kb), (z * 2 + 1 - core, col))

        for t in range(nz + 3):
            if t < nz:
                handle(t, 0, 0)
            if 0 <= t - 1 < nz:
                for ka in range(1, side):
                    handle(t - 1, ka, 0)
            if 0 <= t - 2 < nz:
                for ka in range(side):
                    for kb in range(1, side):
                        handle(t - 2, ka, kb)
            if 0 <= t - 3 < nz:
                for ka in range(side):
                    for kb in range(side):
                        arrive(slot_of(t - 3, kb, ka), 1 - core, nchips + number(t - 3, ka, kb))
                ready((z - (t - 3) + nz) % nz)
        return started

    points = pts_ref[...]
    own32 = points.astype(jnp.float32)
    own_sq = jnp.sum(own32 * own32, axis=1, keepdims=True)
    pair = 2 if plane % 2 == 0 else 1
    wide = pair * 2 * rows

    sums = []

    def make_kernel(zz):
        def body(i, acc):
            block = buf[pl.ds(zz * plane + i * pair, pair), :, :, :width].reshape(wide, width)
            gram = lax.dot_general(points, block, (((1,), (1,)), ((), ())), preferred_element_type=jnp.float32)
            sq = None
            for k in range(0, width, 128):
                piece = block[:, k : k + 128].astype(jnp.float32)
                sq = piece * piece if sq is None else sq + piece * piece
            sq = jnp.sum(sq.T, axis=0, keepdims=True)
            kb = jnp.exp((2.0 * gram - own_sq - sq) * (0.5 / width))
            kern[zz, :, pl.ds(pl.multiple_of(i * wide, wide), wide)] = kb
            return acc + jnp.sum(kb, axis=1, keepdims=True)

        sums.append(lax.fori_loop(0, plane // pair, body, jnp.zeros((rows, 1), jnp.float32)))

    sends = gather(buf, ssem, rsem, make_kernel)
    row_sum = functools.reduce(jnp.add, sums)

    lanes = lax.broadcasted_iota(jnp.int32, (rows, 2 * rows), 1)
    subl = lax.broadcasted_iota(jnp.int32, (rows, 2 * rows), 0)
    spread = jnp.sum(jnp.where(lanes == subl + core * rows, row_sum, 0.0), axis=0, keepdims=True)
    mine = own * 2 + core
    mg[mine] = spread

    def row_sums(kr, kc, sign):
        rr, cc = (row + sign * kr + nrow) % nrow, (col + sign * kc + ncol) % ncol
        k = kr * ncol + kc
        slot = mine if sign > 0 else ((rr // 2) * plane + cc) * 2 + rr % 2
        return pltpu.make_async_remote_copy(
            src_ref=mg.at[slot],
            dst_ref=mg.at[slot],
            send_sem=mssem.at[k],
            recv_sem=mrsem.at[k],
            device_id=(rr, cc),
            device_id_type=MESH,
        )

    def each(action):
        def body(k, carry):
            action(k // ncol, k % ncol)
            return carry

        lax.fori_loop(1, nrow * ncol, body, 0)

    each(lambda kr, kc: row_sums(kr, kc, 1).start())

    def gram_of(load):
        hh = None
        for zz in range(nz):
            hz = load(zz)
            part = lax.dot_general(hz, hz, (((0,), (0,)), ((), ())), preferred_element_type=jnp.float32)
            hh = part if hh is None else hh + part
        return hh

    def load_first(zz):
        return buf[zz * plane : (zz + 1) * plane, :, :, width:].reshape(plane * 2 * rows, rank)

    def load_later(zz):
        return hbuf[zz * plane : (zz + 1) * plane].reshape(plane * 2 * rows, rank)

    def pull(h, hh):
        scale = 0.5 / jnp.sqrt(jnp.sum(hh * hh, keepdims=True) + 1e-06)
        return scale, jnp.dot(h, hh, precision=lax.Precision.HIGHEST, preferred_element_type=jnp.float32)

    scale, hhh = pull(h, gram_of(load_first))
    for op in sends:
        op.wait_send()
    each(lambda kr, kc: row_sums(kr, kc, -1).wait_recv())
    each(lambda kr, kc: row_sums(kr, kc, 1).wait_send())

    grand = jnp.sum(jnp.sum(mg[...], axis=0), axis=1, keepdims=True) / (total * total)
    row_mean = row_sum / total
    shift = grand - row_mean
    ah = jnp.zeros((rows, rank), jnp.float32)
    for zz in range(nz):
        for i in range(plane):
            c = zz * plane + i
            col_mean = (mg[2 * c] + mg[2 * c + 1]) / total
            span = slice(i * 2 * rows, (i + 1) * 2 * rows)
            aff[zz, :, span] = (kern[zz, :, span] - row_mean - col_mean + grand).astype(jnp.bfloat16)
        ah += jnp.dot(aff[zz], load_first(zz), preferred_element_type=jnp.float32)
    h = jnp.maximum(h - scale * (hhh - ah), 0.0)

    hbuf[own, core] = h.astype(jnp.bfloat16)
    partial = []

    def step_two(zz):
        hz = hbuf[pl.ds(zz * plane, plane)].reshape(plane * 2 * rows, rank)
        partial.append(
            (
                jnp.dot(aff[zz], hz, preferred_element_type=jnp.float32),
                lax.dot_general(hz, hz, (((0,), (0,)), ((), ())), preferred_element_type=jnp.float32),
            )
        )

    sends = gather(hbuf, hssem, hrsem, step_two)
    ah = functools.reduce(jnp.add, [p[0] for p in partial])
    scale, hhh = pull(h, functools.reduce(jnp.add, [p[1] for p in partial]))
    out_ref[...] = jnp.maximum(h - scale * (hhh - ah), 0.0) / unit
    for op in sends:
        op.wait_send()


def solution(mesh):
    nrow, ncol = mesh.shape["row"], mesh.shape["col"]
    side = math.isqrt(ncol)
    nz = nrow // 2
    nchips = nz * ncol

    def shards(points, factor):
        rows, width = points.shape
        rank = factor.shape[1]
        return pl.pallas_call(
            functools.partial(kernel, nrow, ncol, side),
            out_shape=jax.ShapeDtypeStruct((rows, rank), jnp.float32),
            in_specs=[pl.BlockSpec(memory_space=pltpu.VMEM)] * 2,
            out_specs=pl.BlockSpec(memory_space=pltpu.VMEM),
            scratch_shapes=[
                pltpu.VMEM((nchips, 2, rows, width + rank), jnp.bfloat16),
                pltpu.VMEM((nchips, 2, rows, rank), jnp.bfloat16),
                pltpu.VMEM((nz, rows, ncol * 2 * rows), jnp.float32),
                pltpu.VMEM((nz, rows, ncol * 2 * rows), jnp.bfloat16),
                pltpu.VMEM((nchips * 2, 1, 2 * rows), jnp.float32),
                pltpu.SemaphoreType.DMA((2 * nchips,)),
                pltpu.SemaphoreType.DMA((2 * nchips,)),
                pltpu.SemaphoreType.DMA((2 * nchips,)),
                pltpu.SemaphoreType.DMA((2 * nchips,)),
                pltpu.SemaphoreType.DMA((nrow * ncol,)),
                pltpu.SemaphoreType.DMA((nrow * ncol,)),
            ],
            compiler_params=pltpu.CompilerParams(
                collective_id=0, has_side_effects=True, vmem_limit_bytes=67043328
            ),
        )(points, factor)

    spec = P(("row", "col"), None)
    return jax.shard_map(shards, mesh=mesh, in_specs=(spec, spec), out_specs=spec, check_vma=False)
```

time: 301 us -> 60.4 us (0.20)
  waiting for transfers between devices: 202 us -> 0 us
  blocking collectives: 65.8 us -> 0 us
  Pallas kernels: 0 us -> 58.8 us
  between operations: 16.6 us -> 0.01 us
  matrix products: 9.39 us -> 0 us
  other arithmetic: 5.03 us -> 0 us
    psum x2 -> x0, waiting for transfers between devices: 202 us -> none  [shards(): hh = lax.psum(local_gram, ('row', 'col'))]
    pallas_call x0 -> x1, Pallas kernels: none -> 58.8 us  [shards(): pl.pallas_call(functools.partial(kernel, nrow, ncol, side), out_shape=jax...]
    all_gather x3 -> x0, blocking collectives: 42.4 us -> none  [the longest x2 32.7 us: shards(): copies = lax.all_gather(hb, 'row', axis=0, tiled=True)]
    psum x2 -> x0, blocking collectives: 23.3 us -> none  [the longest x1 15.8 us: shards(): col_sum, grand = lax.psum((jnp.sum(kern, axis=0), band), 'row')]
    dot_general x7 -> x0, matrix products: 9.39 us -> none  [the longest x2 3.16 us: shards(): lax.dot_general(h, h, (((0,), (0,)), ((), ())), precision=lax.Precision.H...]
    reduce_sum x4 -> x0, other arithmetic: 5.02 us -> none  [the longest x2 3.24 us: shards(): scale = 0.5 / jnp.sqrt(jnp.sum(hh * hh) + 1e-06)]
  transfers between devices with their start and end apart: 5 -> 0, of which waited for: 2 -> 0; matrix products, arithmetic and copies ran while one was open for 3% -> 0% of each run, Pallas kernels for 0% -> 0%
where the time goes in v1:
time: 60.4 us; the launch traced here: 60.3 us
  Pallas kernels  58.8 us (97%)
  local copies, waits for them, and re-layouts  1.47 us (2%)
    pallas_call x1, Pallas kernels, shards(): pl.pallas_call(functools.partial(kernel, nrow, ncol, side), out_shape=jax...  58.8 us
    unnamed x1, local copies, waits for them, and re-layouts  1.47 us

profile of v1, /device:TPU:1, one launch (start us, length us, event | category | flops | bytes accessed | tf_op | source)
XLA Modules:
  0.0 60.3 jit_solution(15926712909370093101)
XLA Ops:
  0.0 58.8 %shard_map.28 = f32[64,256]{1,0:T(8,128)} custom-call(bf16[64,1024]{1,0:T(8,128)(2,1)} %pts_ref.1, f32[64,256]{1,0:T(8,128)} %fac_ref.1), custom_call_target="tpu_custom_call" | custom-call | tf_op jit(solution)/shard_map/pallas_call | solution.py:238
  58.8 1.5 %copy.4 = f32[64,256]{1,0:T(8,128)} copy(f32[64,256]{1,0:T(8,128)} %shard_map.28) | data formatting | bytes 131072

commit v2 on v0

v2 whole, which is shorter than its diff:
```python
import functools
import math

import jax
import jax.numpy as jnp
from jax import lax
from jax.experimental import pallas as pl
from jax.experimental.pallas import tpu as pltpu
from jax.sharding import PartitionSpec as P

MESH = pl.DeviceIdType.MESH
EARLY = 3


def kernel(nrow, ncol, side, pts_ref, fac_ref, out_ref, rbuf, cbuf, first, later, kern, asend, arecv, rsum, csum, tsum, sems):
    nz, plane = nrow // 2, ncol
    rows, width = pts_ref.shape
    rank = fac_ref.shape[1]
    total = rows * nrow * ncol
    unit = 2.0 / math.sqrt(total * rank)
    row, col = lax.axis_index("row"), lax.axis_index("col")
    z, core = row // 2, row % 2
    y, x = col // side, col % side
    partner = (z * 2 + 1 - core, col)

    def at(kz, ka, kb, sign):
        ky = ka * (1 - core) + kb * core
        kx = ka * core + kb * (1 - core)
        zz = (z + sign * kz + nz) % nz
        yy = (y + sign * ky + side) % side
        xx = (x + sign * kx + side) % side
        return zz, yy * side + xx

    def number(kz, ka, kb):
        return (kz * side + ka) * side + kb

    def remote(src, dst, pair, index, device):
        return pltpu.make_async_remote_copy(
            src_ref=src,
            dst_ref=dst,
            send_sem=pair[0].at[index],
            recv_sem=pair[1].at[index],
            device_id=device,
            device_id_type=MESH,
        )

    started = []

    def send(block, pair, index, device):
        op = remote(block, block, pair, index, device)
        op.start()
        started.append(op)

    def arrive(block, pair, index):
        remote(block, block, pair, index, partner).wait_recv()

    barrier = pltpu.get_barrier_semaphore()
    steps = range(1, side)
    peers = [(kz, 0, 0) for kz in range(1, nz)] + [(0, k, 0) for k in steps] + [(0, 0, k) for k in steps]
    for peer in peers:
        zz, cc = at(*peer, 1)
        pl.semaphore_signal(barrier, inc=1, device_id=(zz * 2 + core, cc), device_id_type=MESH)
    pl.semaphore_signal(barrier, inc=1, device_id=partner, device_id_type=MESH)

    h = fac_ref[...] * unit
    rbuf[col] = pts_ref[...]
    cbuf[z, core] = pts_ref[...]
    first[col, z, core] = h.astype(jnp.bfloat16)
    pl.semaphore_wait(barrier, len(peers) + 1)

    def gather(ref, pair):
        nchips = nz * plane

        def handle(kz, ka, kb):
            zz, cc = at(kz, ka, kb, -1)
            block = ref.at[cc, zz, core]
            if kz or ka or kb:
                arrive(block, pair, number(kz, ka, kb))
            else:
                for k in range(1, nz):
                    there, _ = at(k, 0, 0, 1)
                    send(block, pair, number(k, 0, 0), (there * 2 + core, col))
            if not kb:
                if not ka:
                    for k in steps:
                        _, there = at(0, k, 0, 1)
                        send(block, pair, number(kz, k, 0), (row, there))
                for k in steps:
                    _, there = at(0, 0, k, 1)
                    send(block, pair, number(kz, ka, k), (row, there))
            send(block, pair, nchips + number(kz, ka, kb), partner)

        def stage(t):
            if t < nz:
                handle(t, 0, 0)
            if 0 <= t - 1 < nz:
                for ka in steps:
                    handle(t - 1, ka, 0)
            if 0 <= t - 2 < nz:
                for ka in range(side):
                    for kb in steps:
                        handle(t - 2, ka, kb)
            if 0 <= t - 3 < nz:
                for ka in range(side):
                    for kb in range(side):
                        zz, cc = at(t - 3, kb, ka, -1)
                        arrive(ref.at[cc, zz, 1 - core], pair, nchips + number(t - 3, ka, kb))
                return (z - (t - 3) + nz) % nz
            return None

        return stage

    zpair, ppair = sems[0], sems[1]
    for k in range(1, nz):
        there, _ = at(k, 0, 0, 1)
        send(cbuf.at[z, core], zpair, k, (there * 2 + core, col))
    for k in steps:
        _, there = at(0, k, 0, 1)
        send(rbuf.at[col], ppair, number(0, k, 0), (row, there))
    for k in steps:
        _, there = at(0, 0, k, 1)
        send(rbuf.at[col], ppair, number(0, 0, k), (row, there))
    send(cbuf.at[z, core], zpair, nz, partner)
    for ka in steps:
        _, cc = at(0, ka, 0, -1)
        arrive(rbuf.at[cc], ppair, number(0, ka, 0))
        for k in steps:
            _, there = at(0, 0, k, 1)
            send(rbuf.at[cc], ppair, number(0, ka, k), (row, there))
    for ka in range(side):
        for kb in steps:
            _, cc = at(0, ka, kb, -1)
            arrive(rbuf.at[cc], ppair, number(0, ka, kb))

    def squares(block):
        acc = None
        for k in range(0, width, 128):
            piece = block[:, k : k + 128].astype(jnp.float32)
            acc = piece * piece if acc is None else acc + piece * piece
        return acc

    band, wide = plane * rows, 2 * rows
    tall = min(band, 256)
    row_acc = [None] * (band // tall)
    row_sq = []
    for r in range(band // tall):
        group = tall // rows
        row_sq.append(jnp.sum(squares(rbuf[r * group : (r + 1) * group].reshape(tall, width)), axis=1, keepdims=True))
    mine = row
    tot = jnp.zeros((1, wide), jnp.float32)
    for kz in range(nz):
        zz = (z - kz + nz) % nz
        if kz:
            arrive(cbuf.at[zz, core], zpair, kz)
            send(cbuf.at[zz, core], zpair, nz + kz, partner)
        arrive(cbuf.at[zz, 1 - core], zpair, nz + kz)
        block = cbuf[zz].reshape(wide, width)
        col_sq = jnp.sum(squares(block).T, axis=0, keepdims=True)
        col_acc = jnp.zeros((1, wide), jnp.float32)
        for r in range(band // tall):
            group = tall // rows
            mat = rbuf[r * group : (r + 1) * group].reshape(tall, width)
            gram = lax.dot_general(mat, block, (((1,), (1,)), ((), ())), preferred_element_type=jnp.float32)
            k = jnp.exp((2.0 * gram - row_sq[r] - col_sq) * (0.5 / width))
            kern[zz, r * tall : (r + 1) * tall, :] = k
            row_acc[r] = k if row_acc[r] is None else row_acc[r] + k
            col_acc += jnp.sum(k, axis=0, keepdims=True)
        csum[mine, pl.ds(zz, 1), :] = col_acc
        tot += col_acc
    for r in range(band // tall):
        rsum[col, :, r * tall : (r + 1) * tall] = jnp.sum(row_acc[r].T, axis=0, keepdims=True)
    mydev = row * ncol + col
    tsum[mydev] = tot

    rpair, cpair, tpair = sems[2], sems[3], sems[4]

    def row_copy(k, sign):
        cc = (col + sign * k + ncol) % ncol
        block = rsum.at[col if sign > 0 else cc]
        return remote(block, block, rpair, k, (row, cc))

    def col_copy(k, sign):
        rr = (row + sign * k + nrow) % nrow
        block = csum.at[row if sign > 0 else rr]
        return remote(block, block, cpair, k, (rr, col))

    def tot_copy(k, sign):
        rr, cc = (row + sign * (k // ncol) + nrow) % nrow, (col + sign * (k % ncol) + ncol) % ncol
        block = tsum.at[mydev if sign > 0 else rr * ncol + cc]
        return remote(block, block, tpair, k, (rr, cc))

    def aff_copy(k, sign):
        cc = (col + sign * k + ncol) % ncol
        return remote(asend.at[cc], arecv.at[col if sign > 0 else cc], sems[5], k, (row, cc))

    def each(count, action):
        def body(k, carry):
            action(k)
            return carry

        lax.fori_loop(1, count, body, 0)

    each(ncol, lambda k: row_copy(k, 1).start())
    each(nrow, lambda k: col_copy(k, 1).start())
    each(nrow * ncol, lambda k: tot_copy(k, 1).start())

    def gram_of(block):
        return lax.dot_general(block, block, (((0,), (0,)), ((), ())), preferred_element_type=jnp.float32)

    def pull(h, hh):
        scale = 0.5 / jnp.sqrt(jnp.sum(hh * hh, keepdims=True) + 1e-06)
        return scale, jnp.dot(h, hh, precision=lax.Precision.HIGHEST, preferred_element_type=jnp.float32)

    stage = gather(first, sems[6])
    for t in range(EARLY):
        stage(t)

    each(ncol, lambda k: row_copy(k, -1).wait_recv())
    each(nrow, lambda k: col_copy(k, -1).wait_recv())
    each(nrow * ncol, lambda k: tot_copy(k, -1).wait_recv())
    grand = jnp.sum(jnp.sum(tsum[...], axis=0), axis=1, keepdims=True) / (total * total)
    col_mean = jnp.sum(csum[...], axis=0) / total
    row_mean = jnp.sum(rsum[...], axis=0) / total
    for r in range(band // tall):
        group = tall // rows
        mean_r = jnp.broadcast_to(row_mean[:, r * tall : (r + 1) * tall], (wide, tall)).T
        for zz in range(nz):
            k = kern[zz, r * tall : (r + 1) * tall, :] - mean_r - col_mean[zz : zz + 1, :] + grand
            asend[r * group : (r + 1) * group, zz] = k.astype(jnp.bfloat16).reshape(group, rows, wide)
    arecv[col] = asend[col]
    each(ncol, lambda k: aff_copy(k, 1).start())

    hh = jnp.zeros((rank, rank), jnp.float32)
    for t in range(EARLY, nz + 3):
        stage(t)
    for zz in range(nz):
        hh += gram_of(first[:, zz].reshape(plane * wide, rank))
    scale, hhh = pull(h, hh)
    each(ncol, lambda k: aff_copy(k, -1).wait_recv())

    def panel(zz):
        return jnp.concatenate([arecv[c, zz] for c in range(plane)], axis=1)

    ah = jnp.zeros((rows, rank), jnp.float32)
    for zz in range(nz):
        ah += jnp.dot(panel(zz), first[:, zz].reshape(plane * wide, rank), preferred_element_type=jnp.float32)
    h = jnp.maximum(h - scale * (hhh - ah), 0.0)

    later[col, z, core] = h.astype(jnp.bfloat16)
    stage = gather(later, sems[7])
    ah = jnp.zeros((rows, rank), jnp.float32)
    hh = jnp.zeros((rank, rank), jnp.float32)
    for t in range(nz + 3):
        zz = stage(t)
        if zz is not None:
            block = later[:, zz].reshape(plane * wide, rank)
            ah += jnp.dot(panel(zz), block, preferred_element_type=jnp.float32)
            hh += gram_of(block)
    scale, hhh = pull(h, hh)
    out_ref[...] = jnp.maximum(h - scale * (hhh - ah), 0.0) / unit
    for op in started:
        op.wait_send()
    each(ncol, lambda k: row_copy(k, 1).wait_send())
    each(nrow, lambda k: col_copy(k, 1).wait_send())
    each(nrow * ncol, lambda k: tot_copy(k, 1).wait_send())
    each(ncol, lambda k: aff_copy(k, 1).wait_send())


def solution(mesh):
    nrow, ncol = mesh.shape["row"], mesh.shape["col"]
    side = math.isqrt(ncol)
    nz = nrow // 2
    nchips = nz * ncol

    def shards(points, factor):
        rows, width = points.shape
        rank = factor.shape[1]
        wide = 2 * rows
        counts = (2 * nz, ncol, ncol, nrow, nrow * ncol, ncol, 2 * nchips, 2 * nchips)
        return pl.pallas_call(
            functools.partial(kernel, nrow, ncol, side),
            out_shape=jax.ShapeDtypeStruct((rows, rank), jnp.float32),
            in_specs=[pl.BlockSpec(memory_space=pltpu.VMEM)] * 2,
            out_specs=pl.BlockSpec(memory_space=pltpu.VMEM),
            scratch_shapes=[
                pltpu.VMEM((ncol, rows, width), jnp.bfloat16),
                pltpu.VMEM((nz, 2, rows, width), jnp.bfloat16),
                pltpu.VMEM((ncol, nz, 2, rows, rank), jnp.bfloat16),
                pltpu.VMEM((ncol, nz, 2, rows, rank), jnp.bfloat16),
                pltpu.VMEM((nz, ncol * rows, wide), jnp.float32),
                pltpu.VMEM((ncol, nz, rows, wide), jnp.bfloat16),
                pltpu.VMEM((ncol, nz, rows, wide), jnp.bfloat16),
                pltpu.VMEM((ncol, 1, ncol * rows), jnp.float32),
                pltpu.VMEM((nrow, nz, wide), jnp.float32),
                pltpu.VMEM((nrow * ncol, 1, wide), jnp.float32),
                [(pltpu.SemaphoreType.DMA((n,)), pltpu.SemaphoreType.DMA((n,))) for n in counts],
            ],
            compiler_params=pltpu.CompilerParams(
                collective_id=0, has_side_effects=True, vmem_limit_bytes=67043328
            ),
        )(points, factor)

    spec = P(("row", "col"), None)
    return jax.shard_map(shards, mesh=mesh, in_specs=(spec, spec), out_specs=spec, check_vma=False)
```

time: 301 us -> 59.4 us (0.20)
  waiting for transfers between devices: 202 us -> 0 us
  blocking collectives: 65.8 us -> 0 us
  Pallas kernels: 0 us -> 57.8 us
  between operations: 16.6 us -> 0.01 us
  matrix products: 9.39 us -> 0 us
  other arithmetic: 5.03 us -> 0 us
    psum x2 -> x0, waiting for transfers between devices: 202 us -> none  [shards(): hh = lax.psum(local_gram, ('row', 'col'))]
    pallas_call x0 -> x1, Pallas kernels: none -> 57.8 us  [shards(): pl.pallas_call(functools.partial(kernel, nrow, ncol, side), out_shape=jax...]
    all_gather x3 -> x0, blocking collectives: 42.4 us -> none  [the longest x2 32.7 us: shards(): copies = lax.all_gather(hb, 'row', axis=0, tiled=True)]
    psum x2 -> x0, blocking collectives: 23.3 us -> none  [the longest x1 15.8 us: shards(): col_sum, grand = lax.psum((jnp.sum(kern, axis=0), band), 'row')]
    dot_general x7 -> x0, matrix products: 9.39 us -> none  [the longest x2 3.16 us: shards(): lax.dot_general(h, h, (((0,), (0,)), ((), ())), precision=lax.Precision.H...]
    reduce_sum x4 -> x0, other arithmetic: 5.02 us -> none  [the longest x2 3.24 us: shards(): scale = 0.5 / jnp.sqrt(jnp.sum(hh * hh) + 1e-06)]
  transfers between devices with their start and end apart: 5 -> 0, of which waited for: 2 -> 0; matrix products, arithmetic and copies ran while one was open for 3% -> 0% of each run, Pallas kernels for 0% -> 0%
where the time goes in v2:
time: 59.4 us; the launch traced here: 59.3 us
  Pallas kernels  57.8 us (97%)
  local copies, waits for them, and re-layouts  1.47 us (2%)
    pallas_call x1, Pallas kernels, shards(): pl.pallas_call(functools.partial(kernel, nrow, ncol, side), out_shape=jax...  57.8 us
    unnamed x1, local copies, waits for them, and re-layouts  1.47 us

profile of v2, /device:TPU:1, one launch (start us, length us, event | category | flops | bytes accessed | tf_op | source)
XLA Modules:
  0.0 59.3 jit_solution(11658711942630620658)
XLA Ops:
  0.0 57.8 %shard_map.28 = f32[64,256]{1,0:T(8,128)} custom-call(bf16[64,1024]{1,0:T(8,128)(2,1)} %pts_ref.1, f32[64,256]{1,0:T(8,128)} %fac_ref.1), custom_call_target="tpu_custom_call" | custom-call | tf_op jit(solution)/shard_map/pallas_call | solution.py:280
  57.8 1.5 %copy.4 = f32[64,256]{1,0:T(8,128)} copy(f32[64,256]{1,0:T(8,128)} %shard_map.28) | data formatting | bytes 131072

commit v3 on v2

--- a/solution.py
+++ b/solution.py
@@ -23,10 +23,20 @@
     y, x = col // side, col % side
     partner = (z * 2 + 1 - core, col)
 
+    def across(kz, sign):
+        if nz & (nz - 1):
+            return (z + sign * kz + nz) % nz
+        zz, bit = z, 1
+        while bit < nz:
+            if kz & bit:
+                zz = zz + bit - 2 * bit * ((z // bit) % 2)
+            bit *= 2
+        return zz
+
     def at(kz, ka, kb, sign):
         ky = ka * (1 - core) + kb * core
         kx = ka * core + kb * (1 - core)
-        zz = (z + sign * kz + nz) % nz
+        zz = across(kz, sign)
         yy = (y + sign * ky + side) % side
         xx = (x + sign * kx + side) % side
         return zz, yy * side + xx
@@ -105,7 +115,7 @@
                     for kb in range(side):
                         zz, cc = at(t - 3, kb, ka, -1)
                         arrive(ref.at[cc, zz, 1 - core], pair, nchips + number(t - 3, ka, kb))
-                return (z - (t - 3) + nz) % nz
+                return across(t - 3, -1)
             return None
 
         return stage
@@ -121,6 +131,8 @@
         _, there = at(0, 0, k, 1)
         send(rbuf.at[col], ppair, number(0, 0, k), (row, there))
     send(cbuf.at[z, core], zpair, nz, partner)
+    stage = gather(first, sems[6])
+    stage(0)
     for ka in steps:
         _, cc = at(0, ka, 0, -1)
         arrive(rbuf.at[cc], ppair, number(0, ka, 0))
@@ -149,10 +161,11 @@
     mine = row
     tot = jnp.zeros((1, wide), jnp.float32)
     for kz in range(nz):
-        zz = (z - kz + nz) % nz
+        zz = across(kz, -1)
         if kz:
             arrive(cbuf.at[zz, core], zpair, kz)
             send(cbuf.at[zz, core], zpair, nz + kz, partner)
+            stage(kz)
         arrive(cbuf.at[zz, 1 - core], zpair, nz + kz)
         block = cbuf[zz].reshape(wide, width)
         col_sq = jnp.sum(squares(block).T, axis=0, keepdims=True)
@@ -211,8 +224,7 @@
         scale = 0.5 / jnp.sqrt(jnp.sum(hh * hh, keepdims=True) + 1e-06)
         return scale, jnp.dot(h, hh, precision=lax.Precision.HIGHEST, preferred_element_type=jnp.float32)
 
-    stage = gather(first, sems[6])
-    for t in range(EARLY):
+    for t in range(nz, nz + EARLY):
         stage(t)
 
     each(ncol, lambda k: row_copy(k, -1).wait_recv())
@@ -231,7 +243,7 @@
     each(ncol, lambda k: aff_copy(k, 1).start())
 
     hh = jnp.zeros((rank, rank), jnp.float32)
-    for t in range(EARLY, nz + 3):
+    for t in range(nz + EARLY, nz + 3):
         stage(t)
     for zz in range(nz):
         hh += gram_of(first[:, zz].reshape(plane * wide, rank))

time: 59.4 us -> 53.9 us (0.907)
  Pallas kernels: 57.8 us -> 52.3 us
    pallas_call x1, Pallas kernels: 57.8 us -> 52.3 us  [shards(): pl.pallas_call(functools.partial(kernel, nrow, ncol, side), out_shape=jax...]
where the time goes in v3:
time: 53.9 us; the launch traced here: 53.8 us
  Pallas kernels  52.3 us (97%)
  local copies, waits for them, and re-layouts  1.47 us (3%)
    pallas_call x1, Pallas kernels, shards(): pl.pallas_call(functools.partial(kernel, nrow, ncol, side), out_shape=jax...  52.3 us
    unnamed x1, local copies, waits for them, and re-layouts  1.47 us

profile of v3, /device:TPU:1, one launch (start us, length us, event | category | flops | bytes accessed | tf_op | source)
XLA Modules:
  0.0 53.8 jit_solution(6280044018921066053)
XLA Ops:
  0.0 52.3 %shard_map.28 = f32[64,256]{1,0:T(8,128)} custom-call(bf16[64,1024]{1,0:T(8,128)(2,1)} %pts_ref.1, f32[64,256]{1,0:T(8,128)} %fac_ref.1), custom_call_target="tpu_custom_call" | custom-call | tf_op jit(solution)/shard_map/pallas_call | solution.py:292
  52.3 1.5 %copy.4 = f32[64,256]{1,0:T(8,128)} copy(f32[64,256]{1,0:T(8,128)} %shard_map.28) | data formatting | bytes 131072

commit v4 on v3

--- a/solution.py
+++ b/solution.py
@@ -9,7 +9,6 @@
 from jax.sharding import PartitionSpec as P
 
 MESH = pl.DeviceIdType.MESH
-EARLY = 3
 
 
 def kernel(nrow, ncol, side, pts_ref, fac_ref, out_ref, rbuf, cbuf, first, later, kern, asend, arecv, rsum, csum, tsum, sems):
@@ -66,7 +65,7 @@
 
     barrier = pltpu.get_barrier_semaphore()
     steps = range(1, side)
-    peers = [(kz, 0, 0) for kz in range(1, nz)] + [(0, k, 0) for k in steps] + [(0, 0, k) for k in steps]
+    peers = [(kz, 0, 0) for kz in range(1, nz)] + [(0, k // side, k % side) for k in range(1, plane)]
     for peer in peers:
         zz, cc = at(*peer, 1)
         pl.semaphore_signal(barrier, inc=1, device_id=(zz * 2 + core, cc), device_id_type=MESH)
@@ -90,14 +89,10 @@
                 for k in range(1, nz):
                     there, _ = at(k, 0, 0, 1)
                     send(block, pair, number(k, 0, 0), (there * 2 + core, col))
-            if not kb:
-                if not ka:
-                    for k in steps:
-                        _, there = at(0, k, 0, 1)
-                        send(block, pair, number(kz, k, 0), (row, there))
-                for k in steps:
-                    _, there = at(0, 0, k, 1)
-                    send(block, pair, number(kz, ka, k), (row, there))
+            if not kb and not ka:
+                for k in range(plane - 1, 0, -1):
+                    _, there = at(0, k // side, k % side, 1)
+                    send(block, pair, number(kz, k // side, k % side), (row, there))
             send(block, pair, nchips + number(kz, ka, kb), partner)
 
         def stage(t):
@@ -121,6 +116,8 @@
         return stage
 
     zpair, ppair = sems[0], sems[1]
+    stage = gather(first, sems[6])
+    stage(0)
     for k in range(1, nz):
         there, _ = at(k, 0, 0, 1)
         send(cbuf.at[z, core], zpair, k, (there * 2 + core, col))
@@ -131,8 +128,7 @@
         _, there = at(0, 0, k, 1)
         send(rbuf.at[col], ppair, number(0, 0, k), (row, there))
     send(cbuf.at[z, core], zpair, nz, partner)
-    stage = gather(first, sems[6])
-    stage(0)
+    stage(1)
     for ka in steps:
         _, cc = at(0, ka, 0, -1)
         arrive(rbuf.at[cc], ppair, number(0, ka, 0))
@@ -160,12 +156,13 @@
         row_sq.append(jnp.sum(squares(rbuf[r * group : (r + 1) * group].reshape(tall, width)), axis=1, keepdims=True))
     mine = row
     tot = jnp.zeros((1, wide), jnp.float32)
+    for t in range(2, nz):
+        stage(t)
     for kz in range(nz):
         zz = across(kz, -1)
         if kz:
             arrive(cbuf.at[zz, core], zpair, kz)
             send(cbuf.at[zz, core], zpair, nz + kz, partner)
-            stage(kz)
         arrive(cbuf.at[zz, 1 - core], zpair, nz + kz)
         block = cbuf[zz].reshape(wide, width)
         col_sq = jnp.sum(squares(block).T, axis=0, keepdims=True)
@@ -217,6 +214,8 @@
     each(nrow, lambda k: col_copy(k, 1).start())
     each(nrow * ncol, lambda k: tot_copy(k, 1).start())
 
+    for t in range(nz, nz+3):
+        stage(t)
     def gram_of(block):
         return lax.dot_general(block, block, (((0,), (0,)), ((), ())), preferred_element_type=jnp.float32)
 
@@ -224,8 +223,6 @@
         scale = 0.5 / jnp.sqrt(jnp.sum(hh * hh, keepdims=True) + 1e-06)
         return scale, jnp.dot(h, hh, precision=lax.Precision.HIGHEST, preferred_element_type=jnp.float32)
 
-    for t in range(nz, nz + EARLY):
-        stage(t)
 
     each(ncol, lambda k: row_copy(k, -1).wait_recv())
     each(nrow, lambda k: col_copy(k, -1).wait_recv())
@@ -243,8 +240,6 @@
     each(ncol, lambda k: aff_copy(k, 1).start())
 
     hh = jnp.zeros((rank, rank), jnp.float32)
-    for t in range(nz + EARLY, nz + 3):
-        stage(t)
     for zz in range(nz):
         hh += gram_of(first[:, zz].reshape(plane * wide, rank))
     scale, hhh = pull(h, hh)

time: 53.9 us -> 51 us (0.946)
  Pallas kernels: 52.3 us -> 49.4 us
    pallas_call x1, Pallas kernels: 52.3 us -> 49.4 us  [shards(): pl.pallas_call(functools.partial(kernel, nrow, ncol, side), out_shape=jax...]
where the time goes in v4:
time: 51 us; the launch traced here: 50.8 us
  Pallas kernels  49.4 us (97%)
  local copies, waits for them, and re-layouts  1.47 us (3%)
    pallas_call x1, Pallas kernels, shards(): pl.pallas_call(functools.partial(kernel, nrow, ncol, side), out_shape=jax...  49.4 us
    unnamed x1, local copies, waits for them, and re-layouts  1.47 us

profile of v4, /device:TPU:1, one launch (start us, length us, event | category | flops | bytes accessed | tf_op | source)
XLA Modules:
  0.0 50.8 jit_solution(13752770921405861052)
XLA Ops:
  0.0 49.4 %shard_map.28 = f32[64,256]{1,0:T(8,128)} custom-call(bf16[64,1024]{1,0:T(8,128)(2,1)} %pts_ref.1, f32[64,256]{1,0:T(8,128)} %fac_ref.1), custom_call_target="tpu_custom_call" | custom-call | tf_op jit(solution)/shard_map/pallas_call | solution.py:287
  49.4 1.5 %copy.4 = f32[64,256]{1,0:T(8,128)} copy(f32[64,256]{1,0:T(8,128)} %shard_map.28) | data formatting | bytes 131072

commit v5 on v4

--- a/solution.py
+++ b/solution.py
@@ -89,11 +89,11 @@
                 for k in range(1, nz):
                     there, _ = at(k, 0, 0, 1)
                     send(block, pair, number(k, 0, 0), (there * 2 + core, col))
+            send(block, pair, nchips + number(kz, ka, kb), partner)
             if not kb and not ka:
                 for k in range(plane - 1, 0, -1):
                     _, there = at(0, k // side, k % side, 1)
                     send(block, pair, number(kz, k // side, k % side), (row, there))
-            send(block, pair, nchips + number(kz, ka, kb), partner)
 
         def stage(t):
             if t < nz:
@@ -208,11 +208,11 @@
             action(k)
             return carry
 
-        lax.fori_loop(1, count, body, 0)
-
+        lax.fori_loop(1, count, body, 0, unroll=count <= 32)
+
+    each(nrow * ncol, lambda k: tot_copy(k, 1).start())
     each(ncol, lambda k: row_copy(k, 1).start())
     each(nrow, lambda k: col_copy(k, 1).start())
-    each(nrow * ncol, lambda k: tot_copy(k, 1).start())
 
     for t in range(nz, nz+3):
         stage(t)

time: 51 us -> 50 us (0.980)
  Pallas kernels: 49.4 us -> 48.3 us
    pallas_call x1, Pallas kernels: 49.4 us -> 48.3 us  [shards(): pl.pallas_call(functools.partial(kernel, nrow, ncol, side), out_shape=jax...]
where the time goes in v5:
time: 50 us; the launch traced here: 49.8 us
  Pallas kernels  48.3 us (97%)
  local copies, waits for them, and re-layouts  1.47 us (3%)
    pallas_call x1, Pallas kernels, shards(): pl.pallas_call(functools.partial(kernel, nrow, ncol, side), out_shape=jax...  48.3 us
    unnamed x1, local copies, waits for them, and re-layouts  1.47 us

profile of v5, /device:TPU:1, one launch (start us, length us, event | category | flops | bytes accessed | tf_op | source)
XLA Modules:
  0.0 49.8 jit_solution(8389244918669989646)
XLA Ops:
  0.0 48.3 %shard_map.28 = f32[64,256]{1,0:T(8,128)} custom-call(bf16[64,1024]{1,0:T(8,128)(2,1)} %pts_ref.1, f32[64,256]{1,0:T(8,128)} %fac_ref.1), custom_call_target="tpu_custom_call" | custom-call | tf_op jit(solution)/shard_map/pallas_call | solution.py:287
  48.3 1.5 %copy.4 = f32[64,256]{1,0:T(8,128)} copy(f32[64,256]{1,0:T(8,128)} %shard_map.28) | data formatting | bytes 131072
